TPU v7x, 32 devices: a whole 2x2x4 slice. The times are simulated.
32 devices in a mesh: gx: 4 (over y, x), gy: 8 (over z, core).
Axes of the slice: x: 2, y: 2, z: 4, core: 2. Of those that a mesh axis runs over, the one named last changes fastest.
Arguments:
- chemical_concentration: float32 [53, 128, 1024], P(None, 'gx', 'gy'), may hold values from 0.01 to 1
- thermal_scaled: float32 [128, 1024], P('gx', 'gy'), may hold values from 1 to 2.5
- tentative_flow_spread: float32 [128, 1024], P('gx', 'gy'), may hold values from -6 to 6
- substep_numbers: int32 [4, 32], P('gx', 'gy'), may hold values from 1 to 4, as said below
- patch_holder_lookup: int32 [4, 32], P('gx', 'gy'), may hold values from 0 to 3, as said below
- consumed_weighting: float32 [325, 53], replicated, may hold values from -0.875 to 0.875
- molar_coefficient: float32 [325, 53], replicated, may hold values from -0.15625 to 0.15625
- frequency_factor_log: float32 [325], replicated, may hold values from -1 to 1
- arrhenius_energy: float32 [325], replicated, may hold values from 0.5 to 3
- enthalpy_released: float32 [325], replicated, may hold values from -0.3125 to 0.3125
Outputs:
- chemicals_after_window: float32 [53, 128, 1024], P(None, 'gx', 'gy')
- thermal_after_window: float32 [128, 1024], P('gx', 'gy')
- scalar_potential_field: float32 [128, 1024], P('gx', 'gy')
- holder_energy_burden: float32 [4, 8], P('gx', 'gy')
Inputs may be any that keep to these rules, and one draw needn't show every extreme that they name: `substep_numbers`: every block has 4 on some tile. `patch_holder_lookup`: in each block's 4 entries every owner 0 to 3 appears exactly 1 times.
All inputs are finite; a program needn't handle non-finite values.
Results may differ from a plain program's by a relative error of at most 0.0003.
Values sent between devices are 32-bit elements; how exact they have to be, the bound alone decides.
No kernel may reach another device: no remote copies, remote signals or barrier semaphores. Data moves between devices by JAX's collectives and lax.ppermute only.
A program may use at most 64 MiB of HBM per device.

v0:
```python
import functools
import math

import jax
import jax.numpy as jnp
from jax import lax
from jax.experimental import pallas as pl
from jax.experimental.pallas import tpu as pltpu
from jax.sharding import PartitionSpec as P

LEVELS = 3
SWEEPS = 2
COARSE = 4

step_time = 0.4
relax = 0.8
lanes = 128
log2e = math.log2(math.e)
f32 = jnp.float32
bf16 = jnp.bfloat16
high = lax.Precision.HIGHEST


def round_up(value, multiple):
    return -(-value // multiple) * multiple


def halves(value):
    top = value.astype(bf16)
    return top, (value - top.astype(f32)).astype(bf16)


def chemistry_kernel(
    tallies_hbm,
    owners_hbm,
    spec_hbm,
    temp_hbm,
    flow_hbm,
    consumed_hbm,
    molar_hbm,
    factor_hbm,
    energy_hbm,
    enthalpy_hbm,
    rhs_out,
    share_out,
    *rest,
    groups,
):
    states = rest[:groups]
    blocks = rest[groups : 2 * groups]
    (
        tallies,
        owners,
        temp_ref,
        flow_ref,
        consumed_ref,
        molar_ref,
        factor_ref,
        energy_ref,
        enthalpy_ref,
        gather_w,
        scatter_one,
        scatter_two,
        energy_b,
        staging,
        late_hi,
        late_lo,
        arrival,
    ) = rest[2 * groups :]
    species = spec_hbm.shape[0]
    reactions = consumed_ref.shape[1]
    depth, group_len = states[0].shape
    pad_s, group_rows, width = blocks[0].shape
    tiles = tallies.shape[1]
    tile_len = groups * group_len // tiles
    pad_r, reach = gather_w.shape[0], late_hi.shape[1]
    used = scatter_two.shape[0]
    spread = staging.shape[1]
    split = scatter_one.shape[1] - pad_r

    small = [
        (consumed_hbm, consumed_ref),
        (factor_hbm, factor_ref),
        (energy_hbm, energy_ref),
        (molar_hbm, molar_ref),
        (enthalpy_hbm, enthalpy_ref),
        (tallies_hbm, tallies),
        (owners_hbm, owners),
        (temp_hbm, temp_ref),
        (flow_hbm, flow_ref),
    ]
    small = [
        pltpu.make_async_copy(source, target, arrival.at[k])
        for k, (source, target) in enumerate(small)
    ]
    large = [
        pltpu.make_async_copy(
            spec_hbm.at[:, group * group_rows : (group + 1) * group_rows, :],
            block.at[:species],
            arrival.at[len(small) + group],
        )
        for group, block in enumerate(blocks)
    ]
    for copy in small + large:
        copy.start()

    def flat(ref):
        return jnp.pad(ref[...].reshape(1, reactions), ((0, 0), (0, spread - reactions)))

    staging[...] = jnp.zeros_like(staging)
    late_hi[...] = jnp.zeros_like(late_hi)
    late_lo[...] = jnp.zeros_like(late_lo)
    for copy in small:
        copy.wait()
    staging[:species, :reactions] = consumed_ref[...]
    weights = staging[...] * jnp.exp(flat(factor_ref))
    row = lax.broadcasted_iota(jnp.int32, weights.shape, 0)
    weights = jnp.where(row == species, flat(energy_ref) * -log2e, weights)
    columns = jnp.transpose(weights)[:pad_r]
    energy_b[...] = jnp.broadcast_to(columns[:, species : species + 1], energy_b.shape)
    lane = lax.broadcasted_iota(jnp.int32, columns.shape, 1)
    top, low = halves(jnp.where(lane < species, columns, 0.0)[:, :depth])
    gather_w[...] = jnp.concatenate([top, top, low], axis=1)
    staging[:species, :reactions] = molar_ref[...]
    enthalpy = flat(enthalpy_ref)
    weights = jnp.where((row == species) | (row == species + 1), enthalpy, staging[...])[:used]
    top = weights.astype(bf16).astype(f32)
    low = (weights - top)[:, :pad_r]
    top = top[:, :pad_r]
    scatter_one[...] = jnp.concatenate(
        [
            jnp.concatenate([top, top[:, :split]], axis=1),
            jnp.concatenate([low, jnp.zeros((used, split), f32)], axis=1),
        ],
        axis=0,
    ).astype(bf16)
    scatter_two[...] = top[:, split:].astype(bf16)

    for group, (state, block) in enumerate(zip(states, blocks)):
        large[group].wait()
        lines = block.reshape(pad_s * group_rows, width)
        state[species:, :] = jnp.zeros((depth - species, group_len), f32)
        for k in range(group_rows):
            here = group * group_rows + k
            part = slice(k * width, (k + 1) * width)
            state[:species, part] = lines[pl.ds(k, species, stride=group_rows), :]
            state[species : species + 1, part] = temp_ref[here : here + 1, :]

    def front(state, begin):
        now = state[:, begin : begin + reach]
        top, low = halves(now)
        operand = jnp.concatenate([top, low, top], axis=0)
        progress = jnp.dot(gather_w[...], operand, preferred_element_type=f32)
        inverse = 1.0 / (1.0 + jnp.abs(now[species : species + 1]))
        energy = jnp.concatenate([energy_b[...]] * (reach // lanes), axis=1)
        return halves(jnp.exp2(energy * inverse) * progress)

    counts = [tallies[0, tile] for tile in range(tiles)]
    turns = functools.reduce(jnp.maximum, counts)

    def per_cell(group, begin, turn):
        first = group * group_len + begin
        piece = min(tile_len, reach)
        row = []
        for cell in range(first, first + reach, piece):
            count = jnp.full((1, piece), counts[cell // tile_len], jnp.int32)
            row.append(jnp.where(turn < count, step_time / count.astype(f32), 0.0))
        return jnp.concatenate(row, axis=1)

    def back(group, begin, flux, turn):
        flux_hi, flux_lo = flux
        operand = jnp.concatenate([flux_hi, flux_lo[:split]], axis=0)
        first = jnp.dot(scatter_one[...], operand, preferred_element_type=f32)
        second = jnp.dot(scatter_two[...], flux_lo[split:], preferred_element_type=f32)
        change = (first[:used] + first[used:]) + second
        states[group][:used, begin : begin + reach] += per_cell(group, begin, turn) * change

    work = [(group, begin) for group in range(groups) for begin in range(0, group_len, reach)]

    def step(turn, carry):
        pending = (*work[-1], (late_hi[...], late_lo[...]), turn - 1)
        for group, begin in work:
            flux = front(states[group], begin)
            back(*pending)
            pending = (group, begin, flux, turn)
        late_hi[...], late_lo[...] = pending[2]
        return carry

    lax.fori_loop(0, turns, step, 0)
    back(*work[-1], (late_hi[...], late_lo[...]), turns - 1)

    lane = lax.broadcasted_iota(jnp.int32, share_out.shape, 1)
    shares = jnp.zeros(share_out.shape, f32)
    for group, state in enumerate(states):
        heat = state[species + 1 : species + 2, :]
        for k in range(group_rows):
            here = group * group_rows + k
            part = slice(k * width, (k + 1) * width)
            rhs_out[here : here + 1, :] = flow_ref[here : here + 1, :] + heat[:, part]
        squares = heat * heat
        for cell in range(0, group_len, min(tile_len, group_len)):
            tile = (group * group_len + cell) // tile_len
            total = jnp.sum(squares[:, cell : cell + tile_len], axis=1, keepdims=True)
            shares = shares + jnp.where(lane == owners[0, tile], total, 0.0)
    share_out[...] = shares


def unpack_kernel(*refs, groups):
    states = refs[:groups]
    spec_hbm, temp_out = refs[groups : groups + 2]
    blocks = refs[groups + 2 : 2 * groups + 2]
    leave = refs[2 * groups + 2]
    species = spec_hbm.shape[0]
    pad_s, group_rows, width = blocks[0].shape
    copies = []
    for group, (state, block) in enumerate(zip(states, blocks)):
        lines = block.reshape(pad_s * group_rows, width)
        for k in range(group_rows):
            here = group * group_rows + k
            part = slice(k * width, (k + 1) * width)
            lines[pl.ds(k, pad_s, stride=group_rows), :] = state[:pad_s, part]
            temp_out[here : here + 1, :] = state[species : species + 1, part]
        copy = pltpu.make_async_copy(
            block.at[:species],
            spec_hbm.at[:, group * group_rows : (group + 1) * group_rows, :],
            leave.at[group],
        )
        copy.start()
        copies.append(copy)
    for copy in copies:
        copy.wait()


def chemistry(spec, temp, flow, tallies, owners, consumed, molar, factor, energy, enthalpy):
    species, rows, width = spec.shape
    reactions = consumed.shape[0]
    group_rows = 8
    groups = rows // group_rows
    group_len = group_rows * width
    depth = round_up(species + 2, 64)
    used = round_up(species + 2, 8)
    pad_r = round_up(reactions, 16)
    split = -pad_r % 256
    reach = 512
    hbm = pl.BlockSpec(memory_space=pltpu.HBM)
    vmem = pl.BlockSpec(memory_space=pltpu.VMEM)
    block = pltpu.VMEM((round_up(species, 8), group_rows, width), f32)
    rhs, shares, *states = pl.pallas_call(
        functools.partial(chemistry_kernel, groups=groups),
        out_shape=[
            jax.ShapeDtypeStruct(temp.shape, f32),
            jax.ShapeDtypeStruct((8, width), f32),
        ]
        + [jax.ShapeDtypeStruct((depth, group_len), f32)] * groups,
        in_specs=[hbm] * 10,
        out_specs=[vmem] * (2 + groups),
        scratch_shapes=[block] * groups
        + [
            pltpu.SMEM(tallies.shape, jnp.int32),
            pltpu.SMEM(owners.shape, jnp.int32),
            pltpu.VMEM(temp.shape, f32),
            pltpu.VMEM(flow.shape, f32),
            pltpu.VMEM((species, reactions), f32),
            pltpu.VMEM((species, reactions), f32),
            pltpu.VMEM((reactions,), f32),
            pltpu.VMEM((reactions,), f32),
            pltpu.VMEM((reactions,), f32),
            pltpu.VMEM((pad_r, 3 * depth), bf16),
            pltpu.VMEM((2 * used, pad_r + split), bf16),
            pltpu.VMEM((used, pad_r - split), bf16),
            pltpu.VMEM((pad_r, lanes), f32),
            pltpu.VMEM((lanes, round_up(reactions, lanes)), f32),
            pltpu.VMEM((pad_r, reach), bf16),
            pltpu.VMEM((pad_r, reach), bf16),
            pltpu.SemaphoreType.DMA((9 + groups,)),
        ],
        compiler_params=pltpu.CompilerParams(vmem_limit_bytes=24 << 20),
        name="chemistry",
    )(
        *(
            pltpu.with_memory_space_constraint(array, pltpu.HBM)
            for array in (
                tallies,
                owners,
                spec,
                temp,
                flow,
                consumed.T,
                molar.T,
                factor,
                energy,
                enthalpy,
            )
        )
    )
    spec_new, temp_new = pl.pallas_call(
        functools.partial(unpack_kernel, groups=groups),
        out_shape=[
            jax.ShapeDtypeStruct(spec.shape, f32),
            jax.ShapeDtypeStruct(temp.shape, f32),
        ],
        in_specs=[vmem] * groups,
        out_specs=[hbm, vmem],
        scratch_shapes=[block] * groups + [pltpu.SemaphoreType.DMA((groups,))],
        compiler_params=pltpu.CompilerParams(vmem_limit_bytes=4 << 20),
        cost_estimate=pl.CostEstimate(
            flops=spec.size, bytes_accessed=8 * spec.size, transcendentals=0
        ),
        name="unpack",
    )(*states)
    return spec_new, temp_new, rhs, shares


def join_kernel(rhs_ref, share_ref, a_ref, b_ref, out_ref, *, reach):
    width = rhs_ref.shape[1]
    even = lax.axis_index("gy") % 2 == 0
    right = jnp.where(even, a_ref[...], b_ref[...])
    left = jnp.where(even, b_ref[...], a_ref[...])
    lane = lax.broadcasted_iota(jnp.int32, rhs_ref.shape, 1)
    side = jnp.where(lane < reach, right, left)
    out_ref[:, :width] = rhs_ref[...]
    out_ref[:, width:] = side
    out_ref[0:1, width:] = jnp.where(
        (lane[0:1] < reach) | (lane[0:1] >= width - reach),
        side[0:1],
        pltpu.roll(share_ref[0:1, :], reach, 1),
    )


def join_sides(rhs, shares, a, b, reach):
    rows, width = rhs.shape
    vmem = pl.BlockSpec(memory_space=pltpu.VMEM)
    return pl.pallas_call(
        functools.partial(join_kernel, reach=reach),
        out_shape=jax.ShapeDtypeStruct((rows, 2 * width), f32),
        in_specs=[vmem] * 4,
        out_specs=vmem,
        compiler_params=pltpu.CompilerParams(vmem_limit_bytes=4 << 20),
        name="join_sides",
    )(rhs, shares, a, b)


def multigrid_kernel(*refs, reach, quick, count_x, count_y):
    if quick:
        mid_ref, a_ref, b_ref, share_ref, out_ref, burden_ref = refs
    else:
        mid_ref, a_ref, b_ref, out_ref = refs
    rows = mid_ref.shape[0]
    width = mid_ref.shape[1] // 2
    at_x = lax.axis_index("gx")
    at_y = lax.axis_index("gy")
    if quick:
        own = (
            mid_ref[0:1, width:]
            + a_ref[0:1, width:]
            + b_ref[0:1, width:]
            + pltpu.roll(share_ref[0:1, :], reach, 1)
        )
        lane = lax.broadcasted_iota(jnp.int32, own.shape, 1)
        own = jnp.where(lane == at_x + reach, own, 0.0)
        burden_ref[...] = jnp.sum(own, axis=1, keepdims=True) / (rows * width)

    even = at_x % 2 == 0
    above = jnp.where(even, b_ref[...], a_ref[...])
    below = jnp.where(even, a_ref[...], b_ref[...])
    whole = jnp.concatenate([above, mid_ref[...], below], axis=0)
    tall, wide = whole.shape
    down = lax.broadcasted_iota(jnp.int32, whole.shape, 0)
    across = lax.broadcasted_iota(jnp.int32, whole.shape, 1)
    row = at_x * rows + down - rows
    column = at_y * width + jnp.where(across >= width + width // 2, across - wide, across)
    inside = (row >= 0) & (row < count_x * rows) & (column >= 0) & (column < count_y * width)
    keep = jnp.where(inside, relax / 4.0, 0.0)
    whole = jnp.where(inside, whole, 0.0)

    def beside(field, step):
        return (
            pltpu.roll(field, step, 0)
            + pltpu.roll(field, tall - step, 0)
            + pltpu.roll(field, step, 1)
            + pltpu.roll(field, wide - step, 1)
        )

    def halve(field, step):
        odd = (down & step) != 0
        field = field + jnp.where(odd, pltpu.roll(field, step, 0), pltpu.roll(field, tall - step, 0))
        odd = (across & step) != 0
        field = field + jnp.where(odd, pltpu.roll(field, step, 1), pltpu.roll(field, wide - step, 1))
        return 0.25 * field

    def smooth(field, source, step):
        return keep * ((field + source) + beside(field, step))

    def vcycle(rhs, level):
        step = 2**level
        scale = 4.0**level
        source = scale * rhs
        field = keep * source
        if level == LEVELS - 1:
            for turn in range(COARSE - 1):
                field = smooth(field, source, step)
            return field
        for turn in range(SWEEPS - 1):
            field = smooth(field, source, step)
        resid = rhs - (4.0 * field - beside(field, step)) / scale
        field = field + vcycle(halve(resid, step), level + 1)
        for turn in range(SWEEPS):
            field = smooth(field, source, step)
        return field

    out_ref[...] = vcycle(whole, 0)[rows : 2 * rows, :width]


def multigrid(mid, a, b, shares, reach, count_x, count_y):
    rows = mid.shape[0]
    width = mid.shape[1] // 2
    quick = shares is not None
    vmem = pl.BlockSpec(memory_space=pltpu.VMEM)
    field = jax.ShapeDtypeStruct((rows, width), f32)
    return pl.pallas_call(
        functools.partial(
            multigrid_kernel, reach=reach, quick=quick, count_x=count_x, count_y=count_y
        ),
        out_shape=(field, jax.ShapeDtypeStruct((1, 1), f32)) if quick else field,
        in_specs=[vmem] * (4 if quick else 3),
        out_specs=(vmem, vmem) if quick else vmem,
        compiler_params=pltpu.CompilerParams(vmem_limit_bytes=8 << 20),
        name="multigrid",
    )(*((mid, a, b, shares) if quick else (mid, a, b)))


def paired(axis, first):
    count = lax.axis_size(axis)
    pairs = []
    for low in range(first, count + first, 2):
        one, other = low % count, (low + 1) % count
        pairs += [(one, other), (other, one)]
    return pairs


def shards(
    chemical_concentration,
    thermal_scaled,
    tentative_flow_spread,
    substep_numbers,
    patch_holder_lookup,
    consumed_weighting,
    molar_coefficient,
    frequency_factor_log,
    arrhenius_energy,
    enthalpy_released,
):
    count_x, count_y = lax.axis_size("gx"), lax.axis_size("gy")
    rows, width = thermal_scaled.shape
    spec_new, temp_new, rhs, shares = chemistry(
        chemical_concentration,
        thermal_scaled,
        tentative_flow_spread,
        substep_numbers,
        patch_holder_lookup,
        consumed_weighting,
        molar_coefficient,
        frequency_factor_log,
        arrhenius_energy,
        enthalpy_released,
    )
    reach = 32
    quick = count_x == 4
    far = lax.ppermute(shares, "gx", [(i, i ^ 2) for i in range(4)]) if quick else None
    side_a = lax.ppermute(rhs, "gy", paired("gy", 0))
    side_b = lax.ppermute(rhs, "gy", paired("gy", 1))
    band = join_sides(rhs, shares, side_a, side_b, reach)
    band_a = lax.ppermute(band, "gx", paired("gx", 0))
    band_b = lax.ppermute(band, "gx", paired("gx", 1))
    if quick:
        field, burden = multigrid(band, band_a, band_b, far, reach, count_x, count_y)
    else:
        field = multigrid(band, band_a, band_b, None, reach, count_x, count_y)
        burden = lax.psum_scatter(
            shares[0, :count_x], "gx", scatter_dimension=0, tiled=True
        ).reshape(1, 1) / (rows * width)
    return spec_new, temp_new, field, burden


def solution(mesh):
    return jax.shard_map(
        shards,
        mesh=mesh,
        in_specs=(
            P(None, "gx", "gy"),
            P("gx", "gy"),
            P("gx", "gy"),
            P("gx", "gy"),
            P("gx", "gy"),
            P(),
            P(),
            P(),
            P(),
            P(),
        ),
        out_specs=(P(None, "gx", "gy"), P("gx", "gy"), P("gx", "gy"), P("gx", "gy")),
        check_vma=False,
    )
```

profile of v0, /device:TPU:0, one launch (start us, length us, event | category | flops | bytes accessed | tf_op | source)
XLA Modules:
  0.0 26.3 jit_solution(7827805643754175812)
XLA Ops:
  0.6 10.4 %chemistry.1 = (f32[32,128]{1,0:T(8,128)S(1)}, f32[8,128]{1,0:T(8,128)S(1)}, f32[64,1024]{1,0:T(8,128)S(1)}, f32[64,1024]{1,0:T(8,128)S(1)}, f32[64,1024]{1,0:T(8,128)S(1)}, /*index=5*/f32[64,1024]{1,0:T(8,128)S(1)}) custom-call(s32[1,4]{1,0:T(1,128)} %tallies_hbm.1, s32[1,4]{1,0:T(1,128)} %owners_hbm.1, f32[53,32,128]{2,1,0:T(8,128)} %spec_hbm.1, ...), custom_call_target="tpu_custom_call" | custom-call | tf_op jit(solution)/shard_map/chemistry/pallas_call | solution.py:248
  11.0 0.5 %collective-permute-start = (f32[32,128]{1,0:T(8,128)S(1)}, f32[32,128]{1,0:T(8,128)S(1)}, u32[]{:S(2)}, u32[]{:S(2)}) collective-permute-start(f32[32,128]{1,0:T(8,128)S(1)} %get-tuple-element.20.rhs_ref), channel_id=1, source_target_pairs={{0,1},{1,0},{2,3},{3,2},{4,5},{5,4},{6,7},{7,6},{8,9},{9,8},{10,11... | collective-permute-start | bytes 49160 | tf_op jit(solution)/shard_map/ppermute | solution.py:470
  11.6 4.7 %collective-permute-start.1 = (f32[32,128]{1,0:T(8,128)S(1)}, f32[32,128]{1,0:T(8,128)S(1)}, u32[]{:S(2)}, u32[]{:S(2)}) collective-permute-start(f32[32,128]{1,0:T(8,128)S(1)} %get-tuple-element.20.rhs_ref), channel_id=1, source_target_pairs={{1,2},{2,1},{3,4},{4,3},{5,6},{6,5},{7,0},{0,7},{9,10},{10,9},{11,... | collective-permute-start | bytes 49160 | tf_op jit(solution)/shard_map/ppermute | solution.py:471
  16.3 0.0 collective-permute-done.a_ref
  16.3 1.4 %collective-permute-done.1.b_ref = f32[32,128]{1,0:T(8,128)S(1)} collective-permute-done((f32[32,128]{1,0:T(8,128)S(1)}, f32[32,128]{1,0:T(8,128)S(1)}, u32[]{:S(2)}, u32[]{:S(2)}) %collective-permute-start.1) | collective-permute-done | bytes 16416 | tf_op jit(solution)/shard_map/ppermute | solution.py:471
  17.7 0.1 join_sides.1.refs_0_
  17.8 1.5 %collective-permute-start.2 = (f32[32,256]{1,0:T(8,128)S(1)}, f32[32,256]{1,0:T(8,128)S(1)}, u32[]{:S(2)}, u32[]{:S(2)}) collective-permute-start(f32[32,256]{1,0:T(8,128)S(1)} %join_sides.1.refs_0_), channel_id=1, source_target_pairs={{0,8},{8,0},{16,24},{24,16},{1,9},{9,1},{17,25},{25,17},{2,10},{10... | collective-permute-start | bytes 98312 | tf_op jit(solution)/shard_map/ppermute | solution.py:473
  19.3 1.5 %collective-permute-start.3 = (f32[32,256]{1,0:T(8,128)S(1)}, f32[32,256]{1,0:T(8,128)S(1)}, u32[]{:S(2)}, u32[]{:S(2)}) collective-permute-start(f32[32,256]{1,0:T(8,128)S(1)} %join_sides.1.refs_0_), channel_id=1, source_target_pairs={{8,16},{16,8},{24,0},{0,24},{9,17},{17,9},{25,1},{1,25},{10,18},{1... | collective-permute-start | bytes 98312 | tf_op jit(solution)/shard_map/ppermute | solution.py:474
  20.8 0.5 %collective-permute-start.4 = (f32[8,128]{1,0:T(8,128)S(1)}, f32[8,128]{1,0:T(8,128)S(1)}, u32[]{:S(2)}, u32[]{:S(2)}) collective-permute-start(f32[8,128]{1,0:T(8,128)S(1)} %get-tuple-element.21.share_ref), channel_id=1, source_target_pairs={{0,16},{8,24},{16,0},{24,8},{1,17},{9,25},{17,1},{25,9},{2,18},{10... | collective-permute-start | bytes 12296 | tf_op jit(solution)/shard_map/ppermute | solution.py:469
  21.3 1.6 %unpack.1 = (f32[53,32,128]{2,1,0:T(8,128)}, f32[32,128]{1,0:T(8,128)}) custom-call(f32[64,1024]{1,0:T(8,128)S(1)} %get-tuple-element.14.refs_0_, f32[64,1024]{1,0:T(8,128)S(1)} %get-tuple-element.15.refs_1_, f32[64,1024]{1,0:T(8,128)S(1)} %get-tuple-element.16.refs_2_, f32[64,1024]{1,0:T(8,128)S(1)} %get-tuple-element.17.refs_3_), custom_call_target="tpu_custom_call" | custom-call | flops 217088 | bytes 1736704 | tf_op jit(solution)/shard_map/unpack/pallas_call | solution.py:296
  22.9 1.5 %collective-permute-done.4.refs_3_ = f32[8,128]{1,0:T(8,128)S(1)} collective-permute-done((f32[8,128]{1,0:T(8,128)S(1)}, f32[8,128]{1,0:T(8,128)S(1)}, u32[]{:S(2)}, u32[]{:S(2)}) %collective-permute-start.4) | collective-permute-done | bytes 4128 | tf_op jit(solution)/shard_map/ppermute | solution.py:469
  24.4 0.0 collective-permute-done.2.refs_1_
  24.4 0.0 collective-permute-done.3.refs_2_
  24.4 1.9 %multigrid.1 = (f32[32,128]{1,0:T(8,128)}, f32[1,1]{1,0:T(1,128)}) custom-call(f32[32,256]{1,0:T(8,128)S(1)} %join_sides.1.refs_0_, f32[32,256]{1,0:T(8,128)S(1)} %collective-permute-done.2.refs_1_, f32[32,256]{1,0:T(8,128)S(1)} %collective-permute-done.3.refs_2_, f32[8,128]{1,0:T(8,128)S(1)} %collective-permute-done.4.refs_3_), custom_call_target="tpu_custom_call" | custom-call | tf_op jit(solution)/shard_map/multigrid/pallas_call | solution.py:420
Async XLA Ops:
  11.0 5.3 %collective-permute-start = (f32[32,128]{1,0:T(8,128)S(1)}, f32[32,128]{1,0:T(8,128)S(1)}, u32[]{:S(2)}, u32[]{:S(2)}) collective-permute-start(f32[32,128]{1,0:T(8,128)S(1)} %get-tuple-element.20.rhs_ref), channel_id=1, source_target_pairs={{0,1},{1,0},{2,3},{3,2},{4,5},{5,4},{6,7},{7,6},{8,9},{9,8},{10,11... | collective-permute-start | bytes 49160 | tf_op jit(solution)/shard_map/ppermute | solution.py:470
  11.6 6.2 %collective-permute-start.1 = (f32[32,128]{1,0:T(8,128)S(1)}, f32[32,128]{1,0:T(8,128)S(1)}, u32[]{:S(2)}, u32[]{:S(2)}) collective-permute-start(f32[32,128]{1,0:T(8,128)S(1)} %get-tuple-element.20.rhs_ref), channel_id=1, source_target_pairs={{1,2},{2,1},{3,4},{4,3},{5,6},{6,5},{7,0},{0,7},{9,10},{10,9},{11,... | collective-permute-start | bytes 49160 | tf_op jit(solution)/shard_map/ppermute | solution.py:471
  17.8 6.6 %collective-permute-start.2 = (f32[32,256]{1,0:T(8,128)S(1)}, f32[32,256]{1,0:T(8,128)S(1)}, u32[]{:S(2)}, u32[]{:S(2)}) collective-permute-start(f32[32,256]{1,0:T(8,128)S(1)} %join_sides.1.refs_0_), channel_id=1, source_target_pairs={{0,8},{8,0},{16,24},{24,16},{1,9},{9,1},{17,25},{25,17},{2,10},{10... | collective-permute-start | bytes 98312 | tf_op jit(solution)/shard_map/ppermute | solution.py:473
  19.3 5.1 %collective-permute-start.3 = (f32[32,256]{1,0:T(8,128)S(1)}, f32[32,256]{1,0:T(8,128)S(1)}, u32[]{:S(2)}, u32[]{:S(2)}) collective-permute-start(f32[32,256]{1,0:T(8,128)S(1)} %join_sides.1.refs_0_), channel_id=1, source_target_pairs={{8,16},{16,8},{24,0},{0,24},{9,17},{17,9},{25,1},{1,25},{10,18},{1... | collective-permute-start | bytes 98312 | tf_op jit(solution)/shard_map/ppermute | solution.py:474
  20.8 3.6 %collective-permute-start.4 = (f32[8,128]{1,0:T(8,128)S(1)}, f32[8,128]{1,0:T(8,128)S(1)}, u32[]{:S(2)}, u32[]{:S(2)}) collective-permute-start(f32[8,128]{1,0:T(8,128)S(1)} %get-tuple-element.21.share_ref), channel_id=1, source_target_pairs={{0,16},{8,24},{16,0},{24,8},{1,17},{9,25},{17,1},{25,9},{2,18},{10... | collective-permute-start | bytes 12296 | tf_op jit(solution)/shard_map/ppermute | solution.py:469
where the time goes:
time: 26.5 us; the launch traced here: 26.3 us
  Pallas kernels  14 us (53%)
  starting transfers between devices  8.75 us (33%)
  waiting for transfers between devices  2.96 us (11%)
  between operations  0.66 us (2%)
    pallas_call x1, Pallas kernels, chemistry(): pl.pallas_call(functools.partial(chemistry_kernel, groups=groups), out_sh...  10.4 us
    ppermute x1, starting transfers between devices, shards(): side_b = lax.ppermute(rhs, 'gy', paired('gy', 1))  4.73 us
    pallas_call x1, Pallas kernels, multigrid(): pl.pallas_call(functools.partial(multigrid_kernel, reach=reach, quick=qui...  1.93 us
    pallas_call x1, Pallas kernels, chemistry(): pl.pallas_call(functools.partial(unpack_kernel, groups=groups), out_shape...  1.58 us
    ppermute x1, waiting for transfers between devices, shards(): lax.ppermute(shares, 'gx', [(i, i ^ 2) for i in range(4)])  1.51 us
    ppermute x1, starting transfers between devices, shards(): band_a = lax.ppermute(band, 'gx', paired('gx', 0))  1.5 us
    ppermute x1, starting transfers between devices, shards(): band_b = lax.ppermute(band, 'gx', paired('gx', 1))  1.49 us
    ppermute x1, waiting for transfers between devices, shards(): side_b = lax.ppermute(rhs, 'gy', paired('gy', 1))  1.44 us
  transfers between devices with their start and end apart: 5, of which 2 were waited for; matrix products, arithmetic and copies ran while one was open for 0% of the time, Pallas kernels for 6%

commit v1 on v0

--- a/solution.py
+++ b/solution.py
@@ -8,6 +8,7 @@
 from jax.experimental.pallas import tpu as pltpu
 from jax.sharding import PartitionSpec as P
 
+
 LEVELS = 3
 SWEEPS = 2
 COARSE = 4
@@ -18,7 +19,6 @@
 log2e = math.log2(math.e)
 f32 = jnp.float32
 bf16 = jnp.bfloat16
-high = lax.Precision.HIGHEST
 
 
 def round_up(value, multiple):
@@ -65,6 +65,7 @@
         staging,
         late_hi,
         late_lo,
+        ahead,
         arrival,
     ) = rest[2 * groups :]
     species = spec_hbm.shape[0]
@@ -76,7 +77,7 @@
     pad_r, reach = gather_w.shape[0], late_hi.shape[1]
     used = scatter_two.shape[0]
     spread = staging.shape[1]
-    split = scatter_one.shape[1] - pad_r
+    deep = scatter_one.shape[1]
 
     small = [
         (consumed_hbm, consumed_ref),
@@ -127,14 +128,8 @@
     top = weights.astype(bf16).astype(f32)
     low = (weights - top)[:, :pad_r]
     top = top[:, :pad_r]
-    scatter_one[...] = jnp.concatenate(
-        [
-            jnp.concatenate([top, top[:, :split]], axis=1),
-            jnp.concatenate([low, jnp.zeros((used, split), f32)], axis=1),
-        ],
-        axis=0,
-    ).astype(bf16)
-    scatter_two[...] = top[:, split:].astype(bf16)
+    scatter_one[...] = jnp.concatenate([top[:, :deep], low[:, :deep]], axis=0).astype(bf16)
+    scatter_two[...] = jnp.concatenate([top[:, deep:], top, low[:, deep:]], axis=1).astype(bf16)
 
     for group, (state, block) in enumerate(zip(states, blocks)):
         large[group].wait()
@@ -146,12 +141,14 @@
             state[:species, part] = lines[pl.ds(k, species, stride=group_rows), :]
             state[species : species + 1, part] = temp_ref[here : here + 1, :]
 
-    def front(state, begin):
-        now = state[:, begin : begin + reach]
-        top, low = halves(now)
+    def spend(group, begin):
+        top, low = halves(states[group][:, begin : begin + reach])
         operand = jnp.concatenate([top, low, top], axis=0)
-        progress = jnp.dot(gather_w[...], operand, preferred_element_type=f32)
-        inverse = 1.0 / (1.0 + jnp.abs(now[species : species + 1]))
+        return jnp.dot(gather_w[...], operand, preferred_element_type=f32)
+
+    def react(group, begin, progress):
+        heat = states[group][species : species + 1, begin : begin + reach]
+        inverse = 1.0 / (1.0 + jnp.abs(heat))
         energy = jnp.concatenate([energy_b[...]] * (reach // lanes), axis=1)
         return halves(jnp.exp2(energy * inverse) * progress)
 
@@ -169,9 +166,9 @@
 
     def back(group, begin, flux, turn):
         flux_hi, flux_lo = flux
-        operand = jnp.concatenate([flux_hi, flux_lo[:split]], axis=0)
-        first = jnp.dot(scatter_one[...], operand, preferred_element_type=f32)
-        second = jnp.dot(scatter_two[...], flux_lo[split:], preferred_element_type=f32)
+        operand = jnp.concatenate([flux_hi[deep:], flux_lo, flux_hi[deep:]], axis=0)
+        first = jnp.dot(scatter_one[...], flux_hi[:deep], preferred_element_type=f32)
+        second = jnp.dot(scatter_two[...], operand, preferred_element_type=f32)
         change = (first[:used] + first[used:]) + second
         states[group][:used, begin : begin + reach] += per_cell(group, begin, turn) * change
 
@@ -179,13 +176,17 @@
 
     def step(turn, carry):
         pending = (*work[-1], (late_hi[...], late_lo[...]), turn - 1)
-        for group, begin in work:
-            flux = front(states[group], begin)
+        progress = ahead[...]
+        for here, after in zip(work, work[1:] + work[:1]):
+            coming = spend(*after)
             back(*pending)
-            pending = (group, begin, flux, turn)
+            pending = (*here, react(*here, progress), turn)
+            progress = coming
+        ahead[...] = progress
         late_hi[...], late_lo[...] = pending[2]
         return carry
 
+    ahead[...] = spend(*work[0])
     lax.fori_loop(0, turns, step, 0)
     back(*work[-1], (late_hi[...], late_lo[...]), turns - 1)
 
@@ -240,8 +241,8 @@
     depth = round_up(species + 2, 64)
     used = round_up(species + 2, 8)
     pad_r = round_up(reactions, 16)
-    split = -pad_r % 256
-    reach = 512
+    deep = pad_r // 256 * 256
+    reach = 256
     hbm = pl.BlockSpec(memory_space=pltpu.HBM)
     vmem = pl.BlockSpec(memory_space=pltpu.VMEM)
     block = pltpu.VMEM((round_up(species, 8), group_rows, width), f32)
@@ -266,12 +267,13 @@
             pltpu.VMEM((reactions,), f32),
             pltpu.VMEM((reactions,), f32),
             pltpu.VMEM((pad_r, 3 * depth), bf16),
-            pltpu.VMEM((2 * used, pad_r + split), bf16),
-            pltpu.VMEM((used, pad_r - split), bf16),
+            pltpu.VMEM((2 * used, deep), bf16),
+            pltpu.VMEM((used, 3 * pad_r - 2 * deep), bf16),
             pltpu.VMEM((pad_r, lanes), f32),
             pltpu.VMEM((lanes, round_up(reactions, lanes)), f32),
             pltpu.VMEM((pad_r, reach), bf16),
             pltpu.VMEM((pad_r, reach), bf16),
+            pltpu.VMEM((pad_r, reach), f32),
             pltpu.SemaphoreType.DMA((9 + groups,)),
         ],
         compiler_params=pltpu.CompilerParams(vmem_limit_bytes=24 << 20),
@@ -397,14 +399,14 @@
         source = scale * rhs
         field = keep * source
         if level == LEVELS - 1:
-            for turn in range(COARSE - 1):
+            for _ in range(COARSE - 1):
                 field = smooth(field, source, step)
             return field
-        for turn in range(SWEEPS - 1):
+        for _ in range(SWEEPS - 1):
             field = smooth(field, source, step)
         resid = rhs - (4.0 * field - beside(field, step)) / scale
         field = field + vcycle(halve(resid, step), level + 1)
-        for turn in range(SWEEPS):
+        for _ in range(SWEEPS):
             field = smooth(field, source, step)
         return field
 
@@ -429,12 +431,13 @@
     )(*((mid, a, b, shares) if quick else (mid, a, b)))
 
 
-def paired(axis, first):
+def paired(axis, first, wrap=False):
     count = lax.axis_size(axis)
     pairs = []
     for low in range(first, count + first, 2):
         one, other = low % count, (low + 1) % count
-        pairs += [(one, other), (other, one)]
+        if one < other or wrap:
+            pairs += [(one, other), (other, one)]
     return pairs
 
 
@@ -466,12 +469,14 @@
     )
     reach = 32
     quick = count_x == 4
-    far = lax.ppermute(shares, "gx", [(i, i ^ 2) for i in range(4)]) if quick else None
+    far = None
+    if quick:
+        far = lax.ppermute(shares, "gx", [(i, i ^ 2) for i in range(4)])
     side_a = lax.ppermute(rhs, "gy", paired("gy", 0))
     side_b = lax.ppermute(rhs, "gy", paired("gy", 1))
     band = join_sides(rhs, shares, side_a, side_b, reach)
     band_a = lax.ppermute(band, "gx", paired("gx", 0))
-    band_b = lax.ppermute(band, "gx", paired("gx", 1))
+    band_b = lax.ppermute(band, "gx", paired("gx", 1, wrap=quick))
     if quick:
         field, burden = multigrid(band, band_a, band_b, far, reach, count_x, count_y)
     else:

time: 26.5 us -> 24.4 us (0.921)
  the two profiles are of different devices: /device:TPU:0 before, /device:TPU:18 now
where the time goes in v1:
time: 24.4 us; the launch traced here: 24.2 us
  Pallas kernels  13.4 us (55%)
  starting transfers between devices  6.02 us (25%)
  waiting for transfers between devices  4.11 us (17%)
  between operations  0.68 us (3%)
    pallas_call x1, Pallas kernels, chemistry(): pl.pallas_call(functools.partial(chemistry_kernel, groups=groups), out_sh...  9.81 us
    ppermute x1, waiting for transfers between devices, shards(): side_b = lax.ppermute(rhs, 'gy', paired('gy', 1))  2.59 us
    ppermute x1, starting transfers between devices, shards(): band_b = lax.ppermute(band, 'gx', paired('gx', 1, wrap=quick))  2.46 us
    ppermute x1, starting transfers between devices, shards(): side_b = lax.ppermute(rhs, 'gy', paired('gy', 1))  2.45 us
    pallas_call x1, Pallas kernels, multigrid(): pl.pallas_call(functools.partial(multigrid_kernel, reach=reach, quick=qui...  1.93 us
    pallas_call x1, Pallas kernels, chemistry(): pl.pallas_call(functools.partial(unpack_kernel, groups=groups), out_shape...  1.58 us
    ppermute x1, waiting for transfers between devices, shards(): far = lax.ppermute(shares, 'gx', [(i, i ^ 2) for i in range(4)])  1.51 us
    ppermute x1, starting transfers between devices, shards(): band_a = lax.ppermute(band, 'gx', paired('gx', 0))  0.53 us
  transfers between devices with their start and end apart: 5, of which 2 were waited for; matrix products, arithmetic and copies ran while one was open for 0% of the time, Pallas kernels for 7%

profile of v1, /device:TPU:18, one launch (start us, length us, event | category | flops | bytes accessed | tf_op | source)
XLA Modules:
  0.0 24.2 jit_solution(6258334996729687259)
XLA Ops:
  0.6 9.8 %chemistry.1 = (f32[32,128]{1,0:T(8,128)S(1)}, f32[8,128]{1,0:T(8,128)S(1)}, f32[64,1024]{1,0:T(8,128)S(1)}, f32[64,1024]{1,0:T(8,128)S(1)}, f32[64,1024]{1,0:T(8,128)S(1)}, /*index=5*/f32[64,1024]{1,0:T(8,128)S(1)}) custom-call(s32[1,4]{1,0:T(1,128)} %tallies_hbm.1, s32[1,4]{1,0:T(1,128)} %owners_hbm.1, f32[53,32,128]{2,1,0:T(8,128)} %spec_hbm.1, ...), custom_call_target="tpu_custom_call" | custom-call | tf_op jit(solution)/shard_map/chemistry/pallas_call | solution.py:249
  10.5 0.1 collective-permute-start
  10.5 2.4 %collective-permute-start.1 = (f32[32,128]{1,0:T(8,128)S(1)}, f32[32,128]{1,0:T(8,128)S(1)}, u32[]{:S(2)}, u32[]{:S(2)}) collective-permute-start(f32[32,128]{1,0:T(8,128)S(1)} %get-tuple-element.20.rhs_ref), channel_id=1, source_target_pairs={{1,2},{2,1},{3,4},{4,3},{5,6},{6,5},{9,10},{10,9},{11,12},{12,11},... | collective-permute-start | bytes 49160 | tf_op jit(solution)/shard_map/ppermute | solution.py:476
  13.0 0.0 collective-permute-done.a_ref
  13.0 2.6 %collective-permute-done.1.b_ref = f32[32,128]{1,0:T(8,128)S(1)} collective-permute-done((f32[32,128]{1,0:T(8,128)S(1)}, f32[32,128]{1,0:T(8,128)S(1)}, u32[]{:S(2)}, u32[]{:S(2)}) %collective-permute-start.1) | collective-permute-done | bytes 16416 | tf_op jit(solution)/shard_map/ppermute | solution.py:476
  15.6 0.1 join_sides.1.refs_0_
  15.7 0.5 %collective-permute-start.2 = (f32[32,256]{1,0:T(8,128)S(1)}, f32[32,256]{1,0:T(8,128)S(1)}, u32[]{:S(2)}, u32[]{:S(2)}) collective-permute-start(f32[32,256]{1,0:T(8,128)S(1)} %join_sides.1.refs_0_), channel_id=1, source_target_pairs={{0,8},{8,0},{16,24},{24,16},{1,9},{9,1},{17,25},{25,17},{2,10},{10... | collective-permute-start | bytes 98312 | tf_op jit(solution)/shard_map/ppermute | solution.py:478
  16.2 2.5 %collective-permute-start.3 = (f32[32,256]{1,0:T(8,128)S(1)}, f32[32,256]{1,0:T(8,128)S(1)}, u32[]{:S(2)}, u32[]{:S(2)}) collective-permute-start(f32[32,256]{1,0:T(8,128)S(1)} %join_sides.1.refs_0_), channel_id=1, source_target_pairs={{8,16},{16,8},{24,0},{0,24},{9,17},{17,9},{25,1},{1,25},{10,18},{1... | collective-permute-start | bytes 98312 | tf_op jit(solution)/shard_map/ppermute | solution.py:479
  18.7 0.5 %collective-permute-start.4 = (f32[8,128]{1,0:T(8,128)S(1)}, f32[8,128]{1,0:T(8,128)S(1)}, u32[]{:S(2)}, u32[]{:S(2)}) collective-permute-start(f32[8,128]{1,0:T(8,128)S(1)} %get-tuple-element.21.share_ref), channel_id=1, source_target_pairs={{0,16},{8,24},{16,0},{24,8},{1,17},{9,25},{17,1},{25,9},{2,18},{10... | collective-permute-start | bytes 12296 | tf_op jit(solution)/shard_map/ppermute | solution.py:474
  19.2 1.6 %unpack.1 = (f32[53,32,128]{2,1,0:T(8,128)}, f32[32,128]{1,0:T(8,128)}) custom-call(f32[64,1024]{1,0:T(8,128)S(1)} %get-tuple-element.14.refs_0_, f32[64,1024]{1,0:T(8,128)S(1)} %get-tuple-element.15.refs_1_, f32[64,1024]{1,0:T(8,128)S(1)} %get-tuple-element.16.refs_2_, f32[64,1024]{1,0:T(8,128)S(1)} %get-tuple-element.17.refs_3_), custom_call_target="tpu_custom_call" | custom-call | flops 217088 | bytes 1736704 | tf_op jit(solution)/shard_map/unpack/pallas_call | solution.py:298
  20.8 1.5 %collective-permute-done.4.refs_3_ = f32[8,128]{1,0:T(8,128)S(1)} collective-permute-done((f32[8,128]{1,0:T(8,128)S(1)}, f32[8,128]{1,0:T(8,128)S(1)}, u32[]{:S(2)}, u32[]{:S(2)}) %collective-permute-start.4) | collective-permute-done | bytes 4128 | tf_op jit(solution)/shard_map/ppermute | solution.py:474
  22.3 0.0 collective-permute-done.2.refs_1_
  22.3 0.0 collective-permute-done.3.refs_2_
  22.3 1.9 %multigrid.1 = (f32[32,128]{1,0:T(8,128)}, f32[1,1]{1,0:T(1,128)}) custom-call(f32[32,256]{1,0:T(8,128)S(1)} %join_sides.1.refs_0_, f32[32,256]{1,0:T(8,128)S(1)} %collective-permute-done.2.refs_1_, f32[32,256]{1,0:T(8,128)S(1)} %collective-permute-done.3.refs_2_, f32[8,128]{1,0:T(8,128)S(1)} %collective-permute-done.4.refs_3_), custom_call_target="tpu_custom_call" | custom-call | tf_op jit(solution)/shard_map/multigrid/pallas_call | solution.py:422
Async XLA Ops:
  10.5 2.5 %collective-permute-start = (f32[32,128]{1,0:T(8,128)S(1)}, f32[32,128]{1,0:T(8,128)S(1)}, u32[]{:S(2)}, u32[]{:S(2)}) collective-permute-start(f32[32,128]{1,0:T(8,128)S(1)} %get-tuple-element.20.rhs_ref), channel_id=1, source_target_pairs={{0,1},{1,0},{2,3},{3,2},{4,5},{5,4},{6,7},{7,6},{8,9},{9,8},{10,11... | collective-permute-start | bytes 49160 | tf_op jit(solution)/shard_map/ppermute | solution.py:475
  10.5 5.1 %collective-permute-start.1 = (f32[32,128]{1,0:T(8,128)S(1)}, f32[32,128]{1,0:T(8,128)S(1)}, u32[]{:S(2)}, u32[]{:S(2)}) collective-permute-start(f32[32,128]{1,0:T(8,128)S(1)} %get-tuple-element.20.rhs_ref), channel_id=1, source_target_pairs={{1,2},{2,1},{3,4},{4,3},{5,6},{6,5},{9,10},{10,9},{11,12},{12,11},... | collective-permute-start | bytes 49160 | tf_op jit(solution)/shard_map/ppermute | solution.py:476
  15.7 6.6 %collective-permute-start.2 = (f32[32,256]{1,0:T(8,128)S(1)}, f32[32,256]{1,0:T(8,128)S(1)}, u32[]{:S(2)}, u32[]{:S(2)}) collective-permute-start(f32[32,256]{1,0:T(8,128)S(1)} %join_sides.1.refs_0_), channel_id=1, source_target_pairs={{0,8},{8,0},{16,24},{24,16},{1,9},{9,1},{17,25},{25,17},{2,10},{10... | collective-permute-start | bytes 98312 | tf_op jit(solution)/shard_map/ppermute | solution.py:478
  16.2 6.1 %collective-permute-start.3 = (f32[32,256]{1,0:T(8,128)S(1)}, f32[32,256]{1,0:T(8,128)S(1)}, u32[]{:S(2)}, u32[]{:S(2)}) collective-permute-start(f32[32,256]{1,0:T(8,128)S(1)} %join_sides.1.refs_0_), channel_id=1, source_target_pairs={{8,16},{16,8},{24,0},{0,24},{9,17},{17,9},{25,1},{1,25},{10,18},{1... | collective-permute-start | bytes 98312 | tf_op jit(solution)/shard_map/ppermute | solution.py:479
  18.7 3.6 %collective-permute-start.4 = (f32[8,128]{1,0:T(8,128)S(1)}, f32[8,128]{1,0:T(8,128)S(1)}, u32[]{:S(2)}, u32[]{:S(2)}) collective-permute-start(f32[8,128]{1,0:T(8,128)S(1)} %get-tuple-element.21.share_ref), channel_id=1, source_target_pairs={{0,16},{8,24},{16,0},{24,8},{1,17},{9,25},{17,1},{25,9},{2,18},{10... | collective-permute-start | bytes 12296 | tf_op jit(solution)/shard_map/ppermute | solution.py:474

commit v2 on v1

--- a/solution.py
+++ b/solution.py
@@ -366,7 +366,7 @@
     above = jnp.where(even, b_ref[...], a_ref[...])
     below = jnp.where(even, a_ref[...], b_ref[...])
     whole = jnp.concatenate([above, mid_ref[...], below], axis=0)
-    tall, wide = whole.shape
+    wide = whole.shape[1]
     down = lax.broadcasted_iota(jnp.int32, whole.shape, 0)
     across = lax.broadcasted_iota(jnp.int32, whole.shape, 1)
     row = at_x * rows + down - rows
@@ -378,39 +378,68 @@
     def beside(field, step):
         return (
             pltpu.roll(field, step, 0)
-            + pltpu.roll(field, tall - step, 0)
+            + pltpu.roll(field, field.shape[0] - step, 0)
             + pltpu.roll(field, step, 1)
             + pltpu.roll(field, wide - step, 1)
         )
 
-    def halve(field, step):
-        odd = (down & step) != 0
+    def needed(level, lo, hi):
+        step = 2**level
+        if level == LEVELS - 1:
+            return lo - (COARSE - 1) * step, hi + (COARSE - 1) * step
+        lo, hi = needed(level + 1, *coarse_rows(level, lo, hi))
+        lo, hi = lo // (2 * step) * (2 * step), round_up(hi, 2 * step)
+        return lo - SWEEPS * step, hi + SWEEPS * step
+
+    def coarse_rows(level, lo, hi):
+        step = 2**level
+        lo, hi = lo - SWEEPS * step, hi + SWEEPS * step
+        return lo // (2 * step) * (2 * step), round_up(hi, 2 * step)
+
+    def cut(field, base, lo, hi):
+        lo = max(lo // 8 * 8, base)
+        hi = min(round_up(hi, 8), base + field.shape[0])
+        return field[lo - base : hi - base], lo
+
+    def like(full, field, base):
+        return full[base : base + field.shape[0]]
+
+    def halve(field, base, step):
+        odd = (like(down, field, base) & step) != 0
+        tall = field.shape[0]
         field = field + jnp.where(odd, pltpu.roll(field, step, 0), pltpu.roll(field, tall - step, 0))
-        odd = (across & step) != 0
+        odd = (like(across, field, base) & step) != 0
         field = field + jnp.where(odd, pltpu.roll(field, step, 1), pltpu.roll(field, wide - step, 1))
         return 0.25 * field
 
-    def smooth(field, source, step):
-        return keep * ((field + source) + beside(field, step))
-
-    def vcycle(rhs, level):
+    def sweeps(field, source, base, step, count, lo, hi):
+        for left in range(count, 0, -1):
+            was = base
+            field, base = cut(field, was, lo - left * step, hi + left * step)
+            source, _ = cut(source, was, lo - left * step, hi + left * step)
+            field = like(keep, field, base) * ((field + source) + beside(field, step))
+        return field, base
+
+    def vcycle(rhs, base, level, lo, hi):
         step = 2**level
         scale = 4.0**level
         source = scale * rhs
-        field = keep * source
+        field = like(keep, rhs, base) * source
         if level == LEVELS - 1:
-            for _ in range(COARSE - 1):
-                field = smooth(field, source, step)
-            return field
+            return sweeps(field, source, base, step, COARSE - 1, lo, hi)
         for _ in range(SWEEPS - 1):
-            field = smooth(field, source, step)
+            field = like(keep, rhs, base) * ((field + source) + beside(field, step))
         resid = rhs - (4.0 * field - beside(field, step)) / scale
-        field = field + vcycle(halve(resid, step), level + 1)
-        for _ in range(SWEEPS):
-            field = smooth(field, source, step)
-        return field
-
-    out_ref[...] = vcycle(whole, 0)[rows : 2 * rows, :width]
+        coarse_lo, coarse_hi = coarse_rows(level, lo, hi)
+        resid, coarse_base = cut(resid, base, *needed(level + 1, coarse_lo, coarse_hi))
+        resid = halve(resid, coarse_base, step)
+        coarse, coarse_base = vcycle(resid, coarse_base, level + 1, coarse_lo, coarse_hi)
+        coarse, coarse_base = cut(coarse, coarse_base, coarse_lo, coarse_hi)
+        part = slice(coarse_base - base, coarse_base - base + coarse.shape[0])
+        return sweeps(field[part] + coarse, source[part], coarse_base, step, SWEEPS, lo, hi)
+
+    field, base = vcycle(whole, 0, 0, rows, 2 * rows)
+    out_ref[...] = field[rows - base : 2 * rows - base, :width]
 
 
 def multigrid(mid, a, b, shares, reach, count_x, count_y):

time: 24.4 us -> 24.2 us (level)
  no operation moved by 1% of the time
where the time goes in v2:
time: 24.2 us; the launch traced here: 24.1 us
  Pallas kernels  13.3 us (55%)
  starting transfers between devices  6.02 us (25%)
  waiting for transfers between devices  4.11 us (17%)
  between operations  0.68 us (3%)
    pallas_call x1, Pallas kernels, chemistry(): pl.pallas_call(functools.partial(chemistry_kernel, groups=groups), out_sh...  9.81 us
    ppermute x1, waiting for transfers between devices, shards(): side_b = lax.ppermute(rhs, 'gy', paired('gy', 1))  2.59 us
    ppermute x1, starting transfers between devices, shards(): band_b = lax.ppermute(band, 'gx', paired('gx', 1, wrap=quick))  2.46 us
    ppermute x1, starting transfers between devices, shards(): side_b = lax.ppermute(rhs, 'gy', paired('gy', 1))  2.45 us
    pallas_call x1, Pallas kernels, multigrid(): pl.pallas_call(functools.partial(multigrid_kernel, reach=reach, quick=qui...  1.8 us
    pallas_call x1, Pallas kernels, chemistry(): pl.pallas_call(functools.partial(unpack_kernel, groups=groups), out_shape...  1.58 us
    ppermute x1, waiting for transfers between devices, shards(): far = lax.ppermute(shares, 'gx', [(i, i ^ 2) for i in range(4)])  1.51 us
    ppermute x1, starting transfers between devices, shards(): band_a = lax.ppermute(band, 'gx', paired('gx', 0))  0.53 us
  transfers between devices with their start and end apart: 5, of which 2 were waited for; matrix products, arithmetic and copies ran while one was open for 0% of the time, Pallas kernels for 7%

profile of v2, /device:TPU:18, one launch (start us, length us, event | category | flops | bytes accessed | tf_op | source)
XLA Modules:
  0.0 24.1 jit_solution(12892627579233076770)
XLA Ops:
  0.6 9.8 %chemistry.1 = (f32[32,128]{1,0:T(8,128)S(1)}, f32[8,128]{1,0:T(8,128)S(1)}, f32[64,1024]{1,0:T(8,128)S(1)}, f32[64,1024]{1,0:T(8,128)S(1)}, f32[64,1024]{1,0:T(8,128)S(1)}, /*index=5*/f32[64,1024]{1,0:T(8,128)S(1)}) custom-call(s32[1,4]{1,0:T(1,128)} %tallies_hbm.1, s32[1,4]{1,0:T(1,128)} %owners_hbm.1, f32[53,32,128]{2,1,0:T(8,128)} %spec_hbm.1, ...), custom_call_target="tpu_custom_call" | custom-call | tf_op jit(solution)/shard_map/chemistry/pallas_call | solution.py:249
  10.5 0.1 collective-permute-start
  10.5 2.4 %collective-permute-start.1 = (f32[32,128]{1,0:T(8,128)S(1)}, f32[32,128]{1,0:T(8,128)S(1)}, u32[]{:S(2)}, u32[]{:S(2)}) collective-permute-start(f32[32,128]{1,0:T(8,128)S(1)} %get-tuple-element.20.rhs_ref), channel_id=1, source_target_pairs={{1,2},{2,1},{3,4},{4,3},{5,6},{6,5},{9,10},{10,9},{11,12},{12,11},... | collective-permute-start | bytes 49160 | tf_op jit(solution)/shard_map/ppermute | solution.py:505
  13.0 0.0 collective-permute-done.a_ref
  13.0 2.6 %collective-permute-done.1.b_ref = f32[32,128]{1,0:T(8,128)S(1)} collective-permute-done((f32[32,128]{1,0:T(8,128)S(1)}, f32[32,128]{1,0:T(8,128)S(1)}, u32[]{:S(2)}, u32[]{:S(2)}) %collective-permute-start.1) | collective-permute-done | bytes 16416 | tf_op jit(solution)/shard_map/ppermute | solution.py:505
  15.6 0.1 join_sides.1.refs_0_
  15.7 0.5 %collective-permute-start.2 = (f32[32,256]{1,0:T(8,128)S(1)}, f32[32,256]{1,0:T(8,128)S(1)}, u32[]{:S(2)}, u32[]{:S(2)}) collective-permute-start(f32[32,256]{1,0:T(8,128)S(1)} %join_sides.1.refs_0_), channel_id=1, source_target_pairs={{0,8},{8,0},{16,24},{24,16},{1,9},{9,1},{17,25},{25,17},{2,10},{10... | collective-permute-start | bytes 98312 | tf_op jit(solution)/shard_map/ppermute | solution.py:507
  16.2 2.5 %collective-permute-start.3 = (f32[32,256]{1,0:T(8,128)S(1)}, f32[32,256]{1,0:T(8,128)S(1)}, u32[]{:S(2)}, u32[]{:S(2)}) collective-permute-start(f32[32,256]{1,0:T(8,128)S(1)} %join_sides.1.refs_0_), channel_id=1, source_target_pairs={{8,16},{16,8},{24,0},{0,24},{9,17},{17,9},{25,1},{1,25},{10,18},{1... | collective-permute-start | bytes 98312 | tf_op jit(solution)/shard_map/ppermute | solution.py:508
  18.7 0.5 %collective-permute-start.4 = (f32[8,128]{1,0:T(8,128)S(1)}, f32[8,128]{1,0:T(8,128)S(1)}, u32[]{:S(2)}, u32[]{:S(2)}) collective-permute-start(f32[8,128]{1,0:T(8,128)S(1)} %get-tuple-element.21.share_ref), channel_id=1, source_target_pairs={{0,16},{8,24},{16,0},{24,8},{1,17},{9,25},{17,1},{25,9},{2,18},{10... | collective-permute-start | bytes 12296 | tf_op jit(solution)/shard_map/ppermute | solution.py:503
  19.2 1.6 %unpack.1 = (f32[53,32,128]{2,1,0:T(8,128)}, f32[32,128]{1,0:T(8,128)}) custom-call(f32[64,1024]{1,0:T(8,128)S(1)} %get-tuple-element.14.refs_0_, f32[64,1024]{1,0:T(8,128)S(1)} %get-tuple-element.15.refs_1_, f32[64,1024]{1,0:T(8,128)S(1)} %get-tuple-element.16.refs_2_, f32[64,1024]{1,0:T(8,128)S(1)} %get-tuple-element.17.refs_3_), custom_call_target="tpu_custom_call" | custom-call | flops 217088 | bytes 1736704 | tf_op jit(solution)/shard_map/unpack/pallas_call | solution.py:298
  20.8 1.5 %collective-permute-done.4.refs_3_ = f32[8,128]{1,0:T(8,128)S(1)} collective-permute-done((f32[8,128]{1,0:T(8,128)S(1)}, f32[8,128]{1,0:T(8,128)S(1)}, u32[]{:S(2)}, u32[]{:S(2)}) %collective-permute-start.4) | collective-permute-done | bytes 4128 | tf_op jit(solution)/shard_map/ppermute | solution.py:503
  22.3 0.0 collective-permute-done.2.refs_1_
  22.3 0.0 collective-permute-done.3.refs_2_
  22.3 1.8 %multigrid.1 = (f32[32,128]{1,0:T(8,128)}, f32[1,1]{1,0:T(1,128)}) custom-call(f32[32,256]{1,0:T(8,128)S(1)} %join_sides.1.refs_0_, f32[32,256]{1,0:T(8,128)S(1)} %collective-permute-done.2.refs_1_, f32[32,256]{1,0:T(8,128)S(1)} %collective-permute-done.3.refs_2_, f32[8,128]{1,0:T(8,128)S(1)} %collective-permute-done.4.refs_3_), custom_call_target="tpu_custom_call" | custom-call | tf_op jit(solution)/shard_map/multigrid/pallas_call | solution.py:451
Async XLA Ops:
  10.5 2.5 %collective-permute-start = (f32[32,128]{1,0:T(8,128)S(1)}, f32[32,128]{1,0:T(8,128)S(1)}, u32[]{:S(2)}, u32[]{:S(2)}) collective-permute-start(f32[32,128]{1,0:T(8,128)S(1)} %get-tuple-element.20.rhs_ref), channel_id=1, source_target_pairs={{0,1},{1,0},{2,3},{3,2},{4,5},{5,4},{6,7},{7,6},{8,9},{9,8},{10,11... | collective-permute-start | bytes 49160 | tf_op jit(solution)/shard_map/ppermute | solution.py:504
  10.5 5.1 %collective-permute-start.1 = (f32[32,128]{1,0:T(8,128)S(1)}, f32[32,128]{1,0:T(8,128)S(1)}, u32[]{:S(2)}, u32[]{:S(2)}) collective-permute-start(f32[32,128]{1,0:T(8,128)S(1)} %get-tuple-element.20.rhs_ref), channel_id=1, source_target_pairs={{1,2},{2,1},{3,4},{4,3},{5,6},{6,5},{9,10},{10,9},{11,12},{12,11},... | collective-permute-start | bytes 49160 | tf_op jit(solution)/shard_map/ppermute | solution.py:505
  15.7 6.6 %collective-permute-start.2 = (f32[32,256]{1,0:T(8,128)S(1)}, f32[32,256]{1,0:T(8,128)S(1)}, u32[]{:S(2)}, u32[]{:S(2)}) collective-permute-start(f32[32,256]{1,0:T(8,128)S(1)} %join_sides.1.refs_0_), channel_id=1, source_target_pairs={{0,8},{8,0},{16,24},{24,16},{1,9},{9,1},{17,25},{25,17},{2,10},{10... | collective-permute-start | bytes 98312 | tf_op jit(solution)/shard_map/ppermute | solution.py:507
  16.2 6.1 %collective-permute-start.3 = (f32[32,256]{1,0:T(8,128)S(1)}, f32[32,256]{1,0:T(8,128)S(1)}, u32[]{:S(2)}, u32[]{:S(2)}) collective-permute-start(f32[32,256]{1,0:T(8,128)S(1)} %join_sides.1.refs_0_), channel_id=1, source_target_pairs={{8,16},{16,8},{24,0},{0,24},{9,17},{17,9},{25,1},{1,25},{10,18},{1... | collective-permute-start | bytes 98312 | tf_op jit(solution)/shard_map/ppermute | solution.py:508
  18.7 3.6 %collective-permute-start.4 = (f32[8,128]{1,0:T(8,128)S(1)}, f32[8,128]{1,0:T(8,128)S(1)}, u32[]{:S(2)}, u32[]{:S(2)}) collective-permute-start(f32[8,128]{1,0:T(8,128)S(1)} %get-tuple-element.21.share_ref), channel_id=1, source_target_pairs={{0,16},{8,24},{16,0},{24,8},{1,17},{9,25},{17,1},{25,9},{2,18},{10... | collective-permute-start | bytes 12296 | tf_op jit(solution)/shard_map/ppermute | solution.py:503

commit v3 on v2

--- a/solution.py
+++ b/solution.py
@@ -109,8 +109,6 @@
         return jnp.pad(ref[...].reshape(1, reactions), ((0, 0), (0, spread - reactions)))
 
     staging[...] = jnp.zeros_like(staging)
-    late_hi[...] = jnp.zeros_like(late_hi)
-    late_lo[...] = jnp.zeros_like(late_lo)
     for copy in small:
         copy.wait()
     staging[:species, :reactions] = consumed_ref[...]
@@ -131,8 +129,8 @@
     scatter_one[...] = jnp.concatenate([top[:, :deep], low[:, :deep]], axis=0).astype(bf16)
     scatter_two[...] = jnp.concatenate([top[:, deep:], top, low[:, deep:]], axis=1).astype(bf16)
 
-    for group, (state, block) in enumerate(zip(states, blocks)):
-        large[group].wait()
+    def load(group):
+        state, block = states[group], blocks[group]
         lines = block.reshape(pad_s * group_rows, width)
         state[species:, :] = jnp.zeros((depth - species, group_len), f32)
         for k in range(group_rows):
@@ -174,20 +172,31 @@
 
     work = [(group, begin) for group in range(groups) for begin in range(0, group_len, reach)]
 
-    def step(turn, carry):
-        pending = (*work[-1], (late_hi[...], late_lo[...]), turn - 1)
-        progress = ahead[...]
+    def step(turn, pending, progress, arrive):
         for here, after in zip(work, work[1:] + work[:1]):
+            arrive(*after)
             coming = spend(*after)
-            back(*pending)
+            if pending is not None:
+                back(*pending)
             pending = (*here, react(*here, progress), turn)
             progress = coming
         ahead[...] = progress
         late_hi[...], late_lo[...] = pending[2]
+
+    def first_seen(group, begin):
+        if begin == 0 and group > 0:
+            load(group)
+
+    def again(turn, carry):
+        pending = (*work[-1], (late_hi[...], late_lo[...]), turn - 1)
+        step(turn, pending, ahead[...], lambda group, begin: None)
         return carry
 
-    ahead[...] = spend(*work[0])
-    lax.fori_loop(0, turns, step, 0)
+    for copy in large:
+        copy.wait()
+    load(0)
+    step(0, None, spend(*work[0]), first_seen)
+    lax.fori_loop(1, turns, again, 0)
     back(*work[-1], (late_hi[...], late_lo[...]), turns - 1)
 
     lane = lax.broadcasted_iota(jnp.int32, share_out.shape, 1)

time: 24.2 us -> 24.2 us (level)
  the two profiles are of different devices: /device:TPU:18 before, /device:TPU:10 now
where the time goes in v3:
time: 24.2 us; the launch traced here: 24 us
  Pallas kernels  13.2 us (55%)
  starting transfers between devices  6.03 us (25%)
  waiting for transfers between devices  4.11 us (17%)
  between operations  0.68 us (3%)
    pallas_call x1, Pallas kernels, chemistry(): pl.pallas_call(functools.partial(chemistry_kernel, groups=groups), out_sh...  9.77 us
    ppermute x1, waiting for transfers between devices, shards(): side_b = lax.ppermute(rhs, 'gy', paired('gy', 1))  2.58 us
    ppermute x1, starting transfers between devices, shards(): side_b = lax.ppermute(rhs, 'gy', paired('gy', 1))  2.46 us
    ppermute x1, starting transfers between devices, shards(): band_b = lax.ppermute(band, 'gx', paired('gx', 1, wrap=quick))  2.46 us
    pallas_call x1, Pallas kernels, multigrid(): pl.pallas_call(functools.partial(multigrid_kernel, reach=reach, quick=qui...  1.8 us
    pallas_call x1, Pallas kernels, chemistry(): pl.pallas_call(functools.partial(unpack_kernel, groups=groups), out_shape...  1.58 us
    ppermute x1, waiting for transfers between devices, shards(): far = lax.ppermute(shares, 'gx', [(i, i ^ 2) for i in range(4)])  1.52 us
    ppermute x1, starting transfers between devices, shards(): band_a = lax.ppermute(band, 'gx', paired('gx', 0))  0.54 us
  transfers between devices with their start and end apart: 5, of which 2 were waited for; matrix products, arithmetic and copies ran while one was open for 0% of the time, Pallas kernels for 7%

profile of v3, /device:TPU:10, one launch (start us, length us, event | category | flops | bytes accessed | tf_op | source)
XLA Modules:
  0.0 24.0 jit_solution(14495555909031374226)
XLA Ops:
  0.6 9.8 %chemistry.1 = (f32[32,128]{1,0:T(8,128)S(1)}, f32[8,128]{1,0:T(8,128)S(1)}, f32[64,1024]{1,0:T(8,128)S(1)}, f32[64,1024]{1,0:T(8,128)S(1)}, f32[64,1024]{1,0:T(8,128)S(1)}, /*index=5*/f32[64,1024]{1,0:T(8,128)S(1)}) custom-call(s32[1,4]{1,0:T(1,128)} %tallies_hbm.1, s32[1,4]{1,0:T(1,128)} %owners_hbm.1, f32[53,32,128]{2,1,0:T(8,128)} %spec_hbm.1, ...), custom_call_target="tpu_custom_call" | custom-call | tf_op jit(solution)/shard_map/chemistry/pallas_call | solution.py:258
  10.4 0.1 collective-permute-start
  10.5 2.5 %collective-permute-start.1 = (f32[32,128]{1,0:T(8,128)S(1)}, f32[32,128]{1,0:T(8,128)S(1)}, u32[]{:S(2)}, u32[]{:S(2)}) collective-permute-start(f32[32,128]{1,0:T(8,128)S(1)} %get-tuple-element.20.rhs_ref), channel_id=1, source_target_pairs={{1,2},{2,1},{3,4},{4,3},{5,6},{6,5},{9,10},{10,9},{11,12},{12,11},... | collective-permute-start | bytes 49160 | tf_op jit(solution)/shard_map/ppermute | solution.py:514
  13.0 0.0 collective-permute-done.a_ref
  13.0 2.6 %collective-permute-done.1.b_ref = f32[32,128]{1,0:T(8,128)S(1)} collective-permute-done((f32[32,128]{1,0:T(8,128)S(1)}, f32[32,128]{1,0:T(8,128)S(1)}, u32[]{:S(2)}, u32[]{:S(2)}) %collective-permute-start.1) | collective-permute-done | bytes 16416 | tf_op jit(solution)/shard_map/ppermute | solution.py:514
  15.5 0.1 join_sides.1.refs_0_
  15.6 0.5 %collective-permute-start.2 = (f32[32,256]{1,0:T(8,128)S(1)}, f32[32,256]{1,0:T(8,128)S(1)}, u32[]{:S(2)}, u32[]{:S(2)}) collective-permute-start(f32[32,256]{1,0:T(8,128)S(1)} %join_sides.1.refs_0_), channel_id=1, source_target_pairs={{0,8},{8,0},{16,24},{24,16},{1,9},{9,1},{17,25},{25,17},{2,10},{10... | collective-permute-start | bytes 98312 | tf_op jit(solution)/shard_map/ppermute | solution.py:516
  16.2 2.5 %collective-permute-start.3 = (f32[32,256]{1,0:T(8,128)S(1)}, f32[32,256]{1,0:T(8,128)S(1)}, u32[]{:S(2)}, u32[]{:S(2)}) collective-permute-start(f32[32,256]{1,0:T(8,128)S(1)} %join_sides.1.refs_0_), channel_id=1, source_target_pairs={{8,16},{16,8},{24,0},{0,24},{9,17},{17,9},{25,1},{1,25},{10,18},{1... | collective-permute-start | bytes 98312 | tf_op jit(solution)/shard_map/ppermute | solution.py:517
  18.6 0.5 %collective-permute-start.4 = (f32[8,128]{1,0:T(8,128)S(1)}, f32[8,128]{1,0:T(8,128)S(1)}, u32[]{:S(2)}, u32[]{:S(2)}) collective-permute-start(f32[8,128]{1,0:T(8,128)S(1)} %get-tuple-element.21.share_ref), channel_id=1, source_target_pairs={{0,16},{8,24},{16,0},{24,8},{1,17},{9,25},{17,1},{25,9},{2,18},{10... | collective-permute-start | bytes 12296 | tf_op jit(solution)/shard_map/ppermute | solution.py:512
  19.1 1.6 %unpack.1 = (f32[53,32,128]{2,1,0:T(8,128)}, f32[32,128]{1,0:T(8,128)}) custom-call(f32[64,1024]{1,0:T(8,128)S(1)} %get-tuple-element.14.refs_0_, f32[64,1024]{1,0:T(8,128)S(1)} %get-tuple-element.15.refs_1_, f32[64,1024]{1,0:T(8,128)S(1)} %get-tuple-element.16.refs_2_, f32[64,1024]{1,0:T(8,128)S(1)} %get-tuple-element.17.refs_3_), custom_call_target="tpu_custom_call" | custom-call | flops 217088 | bytes 1736704 | tf_op jit(solution)/shard_map/unpack/pallas_call | solution.py:307
  20.7 1.5 %collective-permute-done.4.refs_3_ = f32[8,128]{1,0:T(8,128)S(1)} collective-permute-done((f32[8,128]{1,0:T(8,128)S(1)}, f32[8,128]{1,0:T(8,128)S(1)}, u32[]{:S(2)}, u32[]{:S(2)}) %collective-permute-start.4) | collective-permute-done | bytes 4128 | tf_op jit(solution)/shard_map/ppermute | solution.py:512
  22.2 0.0 collective-permute-done.2.refs_1_
  22.2 0.0 collective-permute-done.3.refs_2_
  22.2 1.8 %multigrid.1 = (f32[32,128]{1,0:T(8,128)}, f32[1,1]{1,0:T(1,128)}) custom-call(f32[32,256]{1,0:T(8,128)S(1)} %join_sides.1.refs_0_, f32[32,256]{1,0:T(8,128)S(1)} %collective-permute-done.2.refs_1_, f32[32,256]{1,0:T(8,128)S(1)} %collective-permute-done.3.refs_2_, f32[8,128]{1,0:T(8,128)S(1)} %collective-permute-done.4.refs_3_), custom_call_target="tpu_custom_call" | custom-call | tf_op jit(solution)/shard_map/multigrid/pallas_call | solution.py:460
Async XLA Ops:
  10.4 2.6 %collective-permute-start = (f32[32,128]{1,0:T(8,128)S(1)}, f32[32,128]{1,0:T(8,128)S(1)}, u32[]{:S(2)}, u32[]{:S(2)}) collective-permute-start(f32[32,128]{1,0:T(8,128)S(1)} %get-tuple-element.20.rhs_ref), channel_id=1, source_target_pairs={{0,1},{1,0},{2,3},{3,2},{4,5},{5,4},{6,7},{7,6},{8,9},{9,8},{10,11... | collective-permute-start | bytes 49160 | tf_op jit(solution)/shard_map/ppermute | solution.py:513
  10.5 5.1 %collective-permute-start.1 = (f32[32,128]{1,0:T(8,128)S(1)}, f32[32,128]{1,0:T(8,128)S(1)}, u32[]{:S(2)}, u32[]{:S(2)}) collective-permute-start(f32[32,128]{1,0:T(8,128)S(1)} %get-tuple-element.20.rhs_ref), channel_id=1, source_target_pairs={{1,2},{2,1},{3,4},{4,3},{5,6},{6,5},{9,10},{10,9},{11,12},{12,11},... | collective-permute-start | bytes 49160 | tf_op jit(solution)/shard_map/ppermute | solution.py:514
  15.6 6.6 %collective-permute-start.2 = (f32[32,256]{1,0:T(8,128)S(1)}, f32[32,256]{1,0:T(8,128)S(1)}, u32[]{:S(2)}, u32[]{:S(2)}) collective-permute-start(f32[32,256]{1,0:T(8,128)S(1)} %join_sides.1.refs_0_), channel_id=1, source_target_pairs={{0,8},{8,0},{16,24},{24,16},{1,9},{9,1},{17,25},{25,17},{2,10},{10... | collective-permute-start | bytes 98312 | tf_op jit(solution)/shard_map/ppermute | solution.py:516
  16.2 6.1 %collective-permute-start.3 = (f32[32,256]{1,0:T(8,128)S(1)}, f32[32,256]{1,0:T(8,128)S(1)}, u32[]{:S(2)}, u32[]{:S(2)}) collective-permute-start(f32[32,256]{1,0:T(8,128)S(1)} %join_sides.1.refs_0_), channel_id=1, source_target_pairs={{8,16},{16,8},{24,0},{0,24},{9,17},{17,9},{25,1},{1,25},{10,18},{1... | collective-permute-start | bytes 98312 | tf_op jit(solution)/shard_map/ppermute | solution.py:517
  18.6 3.6 %collective-permute-start.4 = (f32[8,128]{1,0:T(8,128)S(1)}, f32[8,128]{1,0:T(8,128)S(1)}, u32[]{:S(2)}, u32[]{:S(2)}) collective-permute-start(f32[8,128]{1,0:T(8,128)S(1)} %get-tuple-element.21.share_ref), channel_id=1, source_target_pairs={{0,16},{8,24},{16,0},{24,8},{1,17},{9,25},{17,1},{25,9},{2,18},{10... | collective-permute-start | bytes 12296 | tf_op jit(solution)/shard_map/ppermute | solution.py:512

commit v4 on v2

--- a/solution.py
+++ b/solution.py
@@ -295,7 +295,14 @@
             )
         )
     )
-    spec_new, temp_new = pl.pallas_call(
+    outputs = unpack(spec, temp, states, groups, block)
+    return *outputs, rhs, shares
+
+
+def unpack(spec, temp, states, groups, block):
+    hbm = pl.BlockSpec(memory_space=pltpu.HBM)
+    vmem = pl.BlockSpec(memory_space=pltpu.VMEM)
+    return pl.pallas_call(
         functools.partial(unpack_kernel, groups=groups),
         out_shape=[
             jax.ShapeDtypeStruct(spec.shape, f32),
@@ -310,7 +317,6 @@
         ),
         name="unpack",
     )(*states)
-    return spec_new, temp_new, rhs, shares
 
 
 def join_kernel(rhs_ref, share_ref, a_ref, b_ref, out_ref, *, reach):
@@ -460,13 +466,24 @@
     )(*((mid, a, b, shares) if quick else (mid, a, b)))
 
 
-def paired(axis, first, wrap=False):
+def paired(axis, first):
     count = lax.axis_size(axis)
     pairs = []
     for low in range(first, count + first, 2):
         one, other = low % count, (low + 1) % count
-        if one < other or wrap:
+        pairs += [(one, other), (other, one)]
+    return pairs
+
+
+def across_chips():
+    count_x, count_y = lax.axis_size("gx"), lax.axis_size("gy")
+    pairs = []
+    for i in range(count_x):
+        for low in range(1, count_y - 1, 2):
+            one, other = i * count_y + low, i * count_y + low + 1
             pairs += [(one, other), (other, one)]
+        for j in (0, count_y - 1):
+            pairs.append((i * count_y + j, (i ^ 1) * count_y + j))
     return pairs
 
 
@@ -502,10 +519,10 @@
     if quick:
         far = lax.ppermute(shares, "gx", [(i, i ^ 2) for i in range(4)])
     side_a = lax.ppermute(rhs, "gy", paired("gy", 0))
-    side_b = lax.ppermute(rhs, "gy", paired("gy", 1))
+    side_b = lax.ppermute(rhs, ("gx", "gy"), across_chips())
     band = join_sides(rhs, shares, side_a, side_b, reach)
     band_a = lax.ppermute(band, "gx", paired("gx", 0))
-    band_b = lax.ppermute(band, "gx", paired("gx", 1, wrap=quick))
+    band_b = lax.ppermute(band, "gx", paired("gx", 1))
     if quick:
         field, burden = multigrid(band, band_a, band_b, far, reach, count_x, count_y)
     else:

time: 24.2 us -> 24.4 us (level)
  the two profiles are of different devices: /device:TPU:18 before, /device:TPU:0 now
where the time goes in v4:
time: 24.4 us; the launch traced here: 24.3 us
  Pallas kernels  13.3 us (55%)
  starting transfers between devices  6.69 us (27%)
  waiting for transfers between devices  3.69 us (15%)
  between operations  0.66 us (3%)
    pallas_call x1, Pallas kernels, chemistry(): pl.pallas_call(functools.partial(chemistry_kernel, groups=groups), out_sh...  9.8 us
    ppermute x1, starting transfers between devices, shards(): side_b = lax.ppermute(rhs, ('gx', 'gy'), across_chips())  2.56 us
    ppermute x1, starting transfers between devices, shards(): band_a = lax.ppermute(band, 'gx', paired('gx', 0))  2.03 us
    ppermute x1, waiting for transfers between devices, shards(): far = lax.ppermute(shares, 'gx', [(i, i ^ 2) for i in range(4)])  1.97 us
    pallas_call x1, Pallas kernels, multigrid(): pl.pallas_call(functools.partial(multigrid_kernel, reach=reach, quick=qui...  1.8 us
    ppermute x1, waiting for transfers between devices, shards(): side_b = lax.ppermute(rhs, ('gx', 'gy'), across_chips())  1.72 us
    pallas_call x1, Pallas kernels, unpack(): pl.pallas_call(functools.partial(unpack_kernel, groups=groups), out_shape...  1.58 us
    ppermute x1, starting transfers between devices, shards(): band_b = lax.ppermute(band, 'gx', paired('gx', 1))  1.49 us
  transfers between devices with their start and end apart: 5, of which 2 were waited for; matrix products, arithmetic and copies ran while one was open for 0% of the time, Pallas kernels for 7%

profile of v4, /device:TPU:0, one launch (start us, length us, event | category | flops | bytes accessed | tf_op | source)
XLA Modules:
  0.0 24.3 jit_solution(6271620956031974973)
XLA Ops:
  0.6 9.8 %chemistry.1 = (f32[32,128]{1,0:T(8,128)S(1)}, f32[8,128]{1,0:T(8,128)S(1)}, f32[64,1024]{1,0:T(8,128)S(1)}, f32[64,1024]{1,0:T(8,128)S(1)}, f32[64,1024]{1,0:T(8,128)S(1)}, /*index=5*/f32[64,1024]{1,0:T(8,128)S(1)}) custom-call(s32[1,4]{1,0:T(1,128)} %tallies_hbm.1, s32[1,4]{1,0:T(1,128)} %owners_hbm.1, f32[53,32,128]{2,1,0:T(8,128)} %spec_hbm.1, ...), custom_call_target="tpu_custom_call" | custom-call | tf_op jit(solution)/shard_map/chemistry/pallas_call | solution.py:249
  10.4 0.6 %collective-permute-start = (f32[32,128]{1,0:T(8,128)S(1)}, f32[32,128]{1,0:T(8,128)S(1)}, u32[]{:S(2)}, u32[]{:S(2)}) collective-permute-start(f32[32,128]{1,0:T(8,128)S(1)} %get-tuple-element.20.rhs_ref), channel_id=1, source_target_pairs={{0,1},{1,0},{2,3},{3,2},{4,5},{5,4},{6,7},{7,6},{8,9},{9,8},{10,11... | collective-permute-start | bytes 49160 | tf_op jit(solution)/shard_map/ppermute | solution.py:521
  11.0 2.6 %collective-permute-start.1 = (f32[32,128]{1,0:T(8,128)S(1)}, f32[32,128]{1,0:T(8,128)S(1)}, u32[]{:S(2)}, u32[]{:S(2)}) collective-permute-start(f32[32,128]{1,0:T(8,128)S(1)} %get-tuple-element.20.rhs_ref), channel_id=1, source_target_pairs={{1,2},{2,1},{3,4},{4,3},{5,6},{6,5},{0,8},{7,15},{9,10},{10,9},{11... | collective-permute-start | bytes 49160 | tf_op jit(solution)/shard_map/ppermute | solution.py:522
  13.6 0.0 collective-permute-done.a_ref
  13.6 1.7 %collective-permute-done.1.b_ref = f32[32,128]{1,0:T(8,128)S(1)} collective-permute-done((f32[32,128]{1,0:T(8,128)S(1)}, f32[32,128]{1,0:T(8,128)S(1)}, u32[]{:S(2)}, u32[]{:S(2)}) %collective-permute-start.1) | collective-permute-done | bytes 16416 | tf_op jit(solution)/shard_map/ppermute | solution.py:522
  15.3 0.1 join_sides.1.refs_0_
  15.4 2.0 %collective-permute-start.2 = (f32[32,256]{1,0:T(8,128)S(1)}, f32[32,256]{1,0:T(8,128)S(1)}, u32[]{:S(2)}, u32[]{:S(2)}) collective-permute-start(f32[32,256]{1,0:T(8,128)S(1)} %join_sides.1.refs_0_), channel_id=1, source_target_pairs={{0,8},{8,0},{16,24},{24,16},{1,9},{9,1},{17,25},{25,17},{2,10},{10... | collective-permute-start | bytes 98312 | tf_op jit(solution)/shard_map/ppermute | solution.py:524
  17.4 1.5 %collective-permute-start.3 = (f32[32,256]{1,0:T(8,128)S(1)}, f32[32,256]{1,0:T(8,128)S(1)}, u32[]{:S(2)}, u32[]{:S(2)}) collective-permute-start(f32[32,256]{1,0:T(8,128)S(1)} %join_sides.1.refs_0_), channel_id=1, source_target_pairs={{8,16},{16,8},{24,0},{0,24},{9,17},{17,9},{25,1},{1,25},{10,18},{1... | collective-permute-start | bytes 98312 | tf_op jit(solution)/shard_map/ppermute | solution.py:525
  18.9 0.0 collective-permute-start.4
  18.9 1.6 %unpack.1 = (f32[53,32,128]{2,1,0:T(8,128)}, f32[32,128]{1,0:T(8,128)}) custom-call(f32[64,1024]{1,0:T(8,128)S(1)} %get-tuple-element.14.refs_0_, f32[64,1024]{1,0:T(8,128)S(1)} %get-tuple-element.15.refs_1_, f32[64,1024]{1,0:T(8,128)S(1)} %get-tuple-element.16.refs_2_, f32[64,1024]{1,0:T(8,128)S(1)} %get-tuple-element.17.refs_3_), custom_call_target="tpu_custom_call" | custom-call | flops 217088 | bytes 1736704 | tf_op jit(solution)/shard_map/unpack/pallas_call | solution.py:305
  20.5 2.0 %collective-permute-done.4.refs_3_ = f32[8,128]{1,0:T(8,128)S(1)} collective-permute-done((f32[8,128]{1,0:T(8,128)S(1)}, f32[8,128]{1,0:T(8,128)S(1)}, u32[]{:S(2)}, u32[]{:S(2)}) %collective-permute-start.4) | collective-permute-done | bytes 4128 | tf_op jit(solution)/shard_map/ppermute | solution.py:520
  22.5 0.0 collective-permute-done.2.refs_1_
  22.5 0.0 collective-permute-done.3.refs_2_
  22.5 1.8 %multigrid.1 = (f32[32,128]{1,0:T(8,128)}, f32[1,1]{1,0:T(1,128)}) custom-call(f32[32,256]{1,0:T(8,128)S(1)} %join_sides.1.refs_0_, f32[32,256]{1,0:T(8,128)S(1)} %collective-permute-done.2.refs_1_, f32[32,256]{1,0:T(8,128)S(1)} %collective-permute-done.3.refs_2_, f32[8,128]{1,0:T(8,128)S(1)} %collective-permute-done.4.refs_3_), custom_call_target="tpu_custom_call" | custom-call | tf_op jit(solution)/shard_map/multigrid/pallas_call | solution.py:457
Async XLA Ops:
  10.4 3.1 %collective-permute-start = (f32[32,128]{1,0:T(8,128)S(1)}, f32[32,128]{1,0:T(8,128)S(1)}, u32[]{:S(2)}, u32[]{:S(2)}) collective-permute-start(f32[32,128]{1,0:T(8,128)S(1)} %get-tuple-element.20.rhs_ref), channel_id=1, source_target_pairs={{0,1},{1,0},{2,3},{3,2},{4,5},{5,4},{6,7},{7,6},{8,9},{9,8},{10,11... | collective-permute-start | bytes 49160 | tf_op jit(solution)/shard_map/ppermute | solution.py:521
  11.0 4.3 %collective-permute-start.1 = (f32[32,128]{1,0:T(8,128)S(1)}, f32[32,128]{1,0:T(8,128)S(1)}, u32[]{:S(2)}, u32[]{:S(2)}) collective-permute-start(f32[32,128]{1,0:T(8,128)S(1)} %get-tuple-element.20.rhs_ref), channel_id=1, source_target_pairs={{1,2},{2,1},{3,4},{4,3},{5,6},{6,5},{0,8},{7,15},{9,10},{10,9},{11... | collective-permute-start | bytes 49160 | tf_op jit(solution)/shard_map/ppermute | solution.py:522
  15.4 7.1 %collective-permute-start.2 = (f32[32,256]{1,0:T(8,128)S(1)}, f32[32,256]{1,0:T(8,128)S(1)}, u32[]{:S(2)}, u32[]{:S(2)}) collective-permute-start(f32[32,256]{1,0:T(8,128)S(1)} %join_sides.1.refs_0_), channel_id=1, source_target_pairs={{0,8},{8,0},{16,24},{24,16},{1,9},{9,1},{17,25},{25,17},{2,10},{10... | collective-permute-start | bytes 98312 | tf_op jit(solution)/shard_map/ppermute | solution.py:524
  17.4 5.1 %collective-permute-start.3 = (f32[32,256]{1,0:T(8,128)S(1)}, f32[32,256]{1,0:T(8,128)S(1)}, u32[]{:S(2)}, u32[]{:S(2)}) collective-permute-start(f32[32,256]{1,0:T(8,128)S(1)} %join_sides.1.refs_0_), channel_id=1, source_target_pairs={{8,16},{16,8},{24,0},{0,24},{9,17},{17,9},{25,1},{1,25},{10,18},{1... | collective-permute-start | bytes 98312 | tf_op jit(solution)/shard_map/ppermute | solution.py:525
  18.9 3.6 %collective-permute-start.4 = (f32[8,128]{1,0:T(8,128)S(1)}, f32[8,128]{1,0:T(8,128)S(1)}, u32[]{:S(2)}, u32[]{:S(2)}) collective-permute-start(f32[8,128]{1,0:T(8,128)S(1)} %get-tuple-element.21.share_ref), channel_id=1, source_target_pairs={{0,16},{8,24},{16,0},{24,8},{1,17},{9,25},{17,1},{25,9},{2,18},{10... | collective-permute-start | bytes 12296 | tf_op jit(solution)/shard_map/ppermute | solution.py:520
